TPU v7x, 512 devices: a whole 4x4x16 slice. The times are simulated.
512 devices in a mesh: seg: 32 (over z_lo, y), blk: 16 (over z_hi, x, core).
Axes of the slice: x: 4, y: 4, z: 16 (z_hi: 2, z_lo: 8; z = z_hi * 8 + z_lo), core: 2. Of those that a mesh axis runs over, the one named last changes fastest.
Arguments:
- queries: float32 [65536, 1024], P(('seg', 'blk')), may hold values from -5 to 5
- keys: float32 [65536, 256], P(('seg', 'blk')), may hold values from -5 to 5
- values: float32 [65536, 256], P(('seg', 'blk')), may hold values from -6 to 6
- gate_logit: float32 [8], replicated, may hold values from -3 to 3
- memory_gain: float32 [1024], replicated, may hold values from 0.5 to 2
Outputs:
- mixed: float32 [65536, 1024], P(('seg', 'blk'))
All inputs are finite; a program needn't handle non-finite values.
Results may differ from a plain program's by a relative error of at most 0.0003.
Values sent between devices are 32-bit elements; how exact they have to be, the bound alone decides.
A program may use at most 64 MiB of HBM per device.

v0:
```python
import jax
import jax.numpy as jnp
from jax import lax
from jax.sharding import PartitionSpec as P

QH = 8
KVH = 2
GROUP = 4
HD = 128
HIGH = lax.Precision.HIGHEST


def side_by_side(arrays, axis, dim, along):
    widths = [a.shape[along] for a in arrays]
    both = jnp.concatenate(arrays, axis=along)
    filled = lax.all_gather(both, axis, axis=dim, tiled=True)
    return tuple(jnp.split(filled, [sum(widths[:k]) for k in range(1, len(widths))], axis=along))


def split_up(shard, dim, peers):
    before, after = (shard.shape[:dim], shard.shape[dim + 1 :])
    return jnp.moveaxis(shard.reshape(*before, peers, -1, *after), dim, 0)


def sent_and_summed(shard, axis, dim):
    peers = lax.axis_size(axis)
    parts = lax.all_to_all(split_up(shard, dim, peers), axis, 0, 0, tiled=True)
    return jnp.sum(parts, axis=0)


def from_everyone(shard, axis):
    copies = jnp.broadcast_to(shard, (lax.axis_size(axis), *shard.shape))
    return lax.all_to_all(copies, axis, split_axis=0, concat_axis=0, tiled=True)


def joined_by_halves(pieces, combine):
    while len(jax.tree.leaves(pieces)[0]) > 1:
        pieces = jax.vmap(combine)(*(pieces[side::2] for side in (0, 1)))
    return pieces[0]


def carried_in(shard, axis, combine, identity):
    peers, index = (lax.axis_size(axis), lax.axis_index(axis))
    passed = jnp.arange(peers) < index

    def kept(part, zero, own):
        part = jnp.where(
            passed.reshape(-1, *(1 for _ in own.shape)), part, jnp.asarray(zero, own.dtype)
        )
        return part

    pieces = from_everyone(shard, axis)
    return joined_by_halves(kept(pieces, identity, shard), combine)


def sigma_map(x):
    return jnp.where(x > 0, x + 1.0, jnp.exp(jnp.minimum(x, 0.0)))


def add_terms(earlier, later):
    return earlier + later


def on_device(queries, keys, values, gate_logit, memory_gain):
    rows = queries.shape[0]
    index = lax.axis_index("blk")
    q_heads = queries.reshape(rows, KVH, GROUP, HD)
    qpos = index * rows + jnp.arange(rows, dtype=jnp.int32)
    scale = 1.0 / jnp.sqrt(jnp.float32(HD))

    def update(carry, pieces):
        top, total, accum = carry
        k_piece, v_piece = pieces
        count = k_piece.shape[0]
        k_h = k_piece.reshape(count, KVH, HD)
        v_h = v_piece.reshape(count, KVH, HD)
        scores = jnp.einsum("rkgd,nkd->kgrn", q_heads, k_h, precision=HIGH) * scale
        kpos = jnp.arange(count, dtype=jnp.int32)
        allowed = (kpos[None, :] <= qpos[:, None])[None, None]
        row_top = jnp.max(jnp.where(allowed, scores, -1e30), axis=-1)
        new_top = jnp.maximum(top, row_top)
        weights = jnp.where(allowed, jnp.exp(scores - new_top[..., None]), 0.0)
        total = jnp.sum(weights, axis=-1)
        accum = jnp.einsum("kgrn,nkd->kgrd", weights, v_h, precision=HIGH)
        return (new_top, total, accum)

    start_state = (
        jnp.full((KVH, GROUP, rows), -1e30, jnp.float32),
        jnp.zeros((KVH, GROUP, rows), jnp.float32),
        jnp.zeros((KVH, GROUP, rows, HD), jnp.float32),
    )
    pieces = side_by_side((keys, values), "blk", 0, 1)
    top, total, accum = lax.cond(
        jnp.int32(0) <= qpos[rows - 1], lambda c: update(c, pieces), lambda c: c, start_state
    )
    attention = accum / total[..., None]
    sig_keys = sigma_map(keys.reshape(rows, KVH, HD))
    partial_value = jnp.einsum(
        "rkd,rke->kde", sig_keys, values.reshape(rows, KVH, HD), precision=HIGH
    ).reshape(KVH * HD, HD)
    shard = sent_and_summed(partial_value, "blk", 0)
    prefix = carried_in(shard, "seg", add_terms, jnp.zeros_like(shard))
    memory = lax.all_gather(prefix, "blk", axis=0, tiled=True)
    retrieval = jnp.einsum(
        "rkgd,kde->kgre", sigma_map(q_heads), memory.reshape(KVH, HD, HD), precision=HIGH
    )
    rms = jnp.sqrt(jnp.mean(retrieval * retrieval, axis=-1, keepdims=True) + 1e-06)
    normed = retrieval / rms * memory_gain.reshape(KVH, GROUP, 1, HD)
    gate = jax.nn.sigmoid(gate_logit).reshape(KVH, GROUP, 1, 1)
    mixed = gate * normed + (1.0 - gate) * attention
    return jnp.transpose(mixed, (2, 0, 1, 3)).reshape(rows, QH * HD)


def solution(mesh):
    return jax.shard_map(
        on_device,
        mesh=mesh,
        in_specs=(
            P(("seg", "blk"), None),
            P(("seg", "blk"), None),
            P(("seg", "blk"), None),
            P(),
            P(),
        ),
        out_specs=P(("seg", "blk"), None),
        check_vma=False,
    )
```

profile of v0, /device:TPU:3, one launch (start us, length us, event | category | flops | bytes accessed | tf_op | source)
XLA Modules:
  0.0 169.8 jit_solution(6998863623988860291)
XLA Ops:
  6.5 0.0 all-gather.3.cloned.1.call-start
  6.5 1.0 copy.19
  7.5 1.0 copy.20
  8.5 0.7 pad_maximum_fusion
  9.3 0.0 all-gather.3.cloned.1.call-update
  9.3 0.9 exponential_select_fusion
  10.2 0.1 copy.34
  10.3 1.2 fusion.19
  11.5 32.2 %all_to_all.10 = f32[16,16,128]{2,1,0:T(8,128)S(1)} all-to-all(f32[16,16,128]{2,1,0:T(8,128)S(1)} %bitcast.56), channel_id=1, replica_groups=mesh['seg'=32,'blk'=16] {'blk'}, dimensions={0} | all-to-all | bytes 262144 | tf_op jit(solution)/shard_map/all_to_all | solution.py:27
  43.8 0.7 broadcast_in_dim.50
  44.5 16.2 %all-to-all-start.1 = ((f32[32,16,128]{2,1,0:T(8,128)}), f32[32,16,128]{2,1,0:T(8,128)S(1)}, u32[]{:S(2)}, u32[]{:S(2)}) async-start(f32[32,16,128]{2,1,0:T(8,128)} %broadcast_in_dim.50), calls=%async_computation.1 | async-start | bytes 524288 | tf_op jit(solution)/shard_map/all_to_all | solution.py:33
  60.7 1.2 copy.16
  61.9 0.6 slice.45
  63.1 0.7 add_divide_fusion
  63.8 0.1 mul.40
  63.9 10.7 %all-to-all-done.1 = f32[32,16,128]{2,1,0:T(8,128)S(1)} async-done(((f32[32,16,128]{2,1,0:T(8,128)}), f32[32,16,128]{2,1,0:T(8,128)S(1)}, u32[]{:S(2)}, u32[]{:S(2)}) %all-to-all-start.1) | async-done | bytes 262176 | tf_op jit(solution)/shard_map/all_to_all | solution.py:33
  74.5 0.1 broadcast_select_fusion
  74.7 59.1 %all-gather = f32[1,256,128]{2,1,0:T(8,128)S(1)} all-gather(f32[1,16,128]{2,1,0:T(8,128)S(1)} %slice_add_fusion.4), channel_id=2, replica_groups=mesh['seg'=32,'blk'=16] {'blk'}, dimensions={1}, use_global_device_ids=true | all-gather | bytes 139264 | tf_op jit(solution)/shard_map/all_gather | solution.py:103
  133.9 0.7 multiply_reduce_fusion
  134.6 8.6 %all-gather.3.cloned.1.call-done = f32[2048,512]{0,1:T(8,128)} async-done(((f32[128,512]{0,1:T(8,128)}), f32[2048,512]{0,1:T(8,128)}) %all-gather.3.cloned.1.call-update) | async-done | bytes 4194320 | tf_op jit(solution)/shard_map/all_gather | solution.py:16
  143.2 0.0 copy-start
  143.2 18.4 %conditional.1 = (f32[2,4,128]{2,1,0:T(4,128)S(1)}, f32[2,4,128,128]{2,3,1,0:T(8,128)S(1)}) conditional(s32[]{:T(128)} %bitcast.12, () %tuple.13, (s32[128]{0:T(128)S(1)}, f32[2048,512]{0,1:T(8,128)}, f32[128,2,4,128]{0,3,2,1:T(8,128)S(1)}) %tuple.25), branch_computations={%region_2.0_spmd, %region_3.6_spmd} | conditional | flops 6463683584 | bytes 39870992 | solution.py:93
  143.2 0.2 iota_compare_fusion
  143.4 2.5 %fusion.24 = (f32[2048,256]{0,1:T(8,128)S(1)}, f32[2048,256]{0,1:T(8,128)S(1)}) fusion(f32[2048,512]{0,1:T(8,128)} %get-tuple-element.15), kind=kLoop, calls=%fused_computation.43 | loop fusion | bytes 8388608 | tf_op jit(solution)/shard_map/split | solution.py:17
  145.9 7.3 %fusion = (f32[2,4,128]{2,1,0:T(4,128)S(1)}, f32[2,2048,128,4]{2,1,3,0:T(8,128)S(1)}) fusion(pred[128,2048]{0,1:T(8,128)(4,1)S(1)} %iota_compare_fusion, f32[2048,2,128,1]{0,2,3,1:T(8,128)S(1)} %bitcast.49, f32[128,2,4,128]{0,3,2,1:T(8,128)S(1)} %get-tuple-element.23), kind=kOutput, calls=%fused_computation.2 | convolution fusion | flops 3227515904 | bytes 11276288 | tf_op jit(solution)/shard_map/cond/branch_1_fun/rkgd,nkd->kgrn/dot_general | solution.py:77
  153.2 6.4 %fusion.3 = f32[2,4,128,128]{2,3,1,0:T(8,128)S(1)} fusion(f32[2048,2,128,1]{0,2,3,1:T(8,128)S(1)} %bitcast.53, f32[2,2048,128,4]{2,1,3,0:T(8,128)S(1)} %get-tuple-element.28, f32[2,4,128]{2,1,0:T(4,128)S(1)} %broadcast_maximum_fusion, pred[128,2048]{0,1:T(8,128)(4,1)S(1)} %iota_compare_fusion), kind=kOutput, calls=%fused_computation.5 | convolution fusion | flops 3227516928 | bytes 11276288 | tf_op jit(solution)/shard_map/cond | solution.py:93
  159.7 1.7 %fusion.5 = f32[2,4,128]{2,1,0:T(4,128)S(1)} fusion(f32[2,2048,128,4]{2,1,3,0:T(8,128)S(1)} %get-tuple-element.28, f32[2,4,128]{2,1,0:T(4,128)S(1)} %broadcast_maximum_fusion, pred[128,2048]{0,1:T(8,128)(4,1)S(1)} %iota_compare_fusion), kind=kLoop, calls=%fused_computation.6 | loop fusion | flops 8387584 | bytes 8658944 | tf_op jit(solution)/shard_map/cond/branch_1_fun/reduce_sum | solution.py:83
  161.7 0.0 copy-done
  161.7 0.2 multiply_add_fusion
  161.9 1.0 copy.23
  (11 shorter events, 0.1 us)
Async XLA Ops:
  6.5 136.7 %all-gather.3.cloned.1.call-start = ((), (), s32[]{:S(2)}) async-start(), calls=%async_computation.2 | async-start | bytes 4456448 | tf_op jit(solution)/shard_map/all_gather | solution.py:16
  44.5 30.1 %all-to-all-start.1 = ((f32[32,16,128]{2,1,0:T(8,128)}), f32[32,16,128]{2,1,0:T(8,128)S(1)}, u32[]{:S(2)}, u32[]{:S(2)}) async-start(f32[32,16,128]{2,1,0:T(8,128)} %broadcast_in_dim.50), calls=%async_computation.1 | async-start | bytes 524288 | tf_op jit(solution)/shard_map/all_to_all | solution.py:33
  143.2 18.5 %copy-start = (f32[1024]{0:T(1024)S(1)}, f32[1024]{0:T(1024)}, u32[]{:S(2)}) copy-start(f32[1024]{0:T(1024)} %param.11) | copy-start | bytes 12292
Sparse Core Ops, SparseCore 0:
  10.5 132.6 all-gather.2
where the time goes:
time: 170 us
  blocking collectives  91.4 us (54%)
  waiting for transfers between devices  19.3 us (11%)
  starting transfers between devices  16.2 us (10%)
  matrix products  15.6 us (9%)
  between operations  14.1 us (8%)
  local copies, waits for them, and re-layouts  8.18 us (5%)
  other arithmetic  4.63 us (3%)
    all_gather x1, blocking collectives, on_device(): memory = lax.all_gather(prefix, 'blk', axis=0, tiled=True)  59.1 us
    all_to_all x1, blocking collectives, sent_and_summed(): parts = lax.all_to_all(split_up(shard, dim, peers), axis, 0, 0, tiled=True)  32.2 us
    all_to_all x1, starting transfers between devices, from_everyone(): return lax.all_to_all(copies, axis, split_axis=0, concat_axis=0, tiled=True)  16.2 us
    all_to_all x1, waiting for transfers between devices, from_everyone(): return lax.all_to_all(copies, axis, split_axis=0, concat_axis=0, tiled=True)  10.7 us
    all_gather x1, waiting for transfers between devices, side_by_side(): filled = lax.all_gather(both, axis, axis=dim, tiled=True)  8.63 us
    dot_general x1, matrix products, update(): scores = jnp.einsum('rkgd,nkd->kgrn', q_heads, k_h, precision=HIGH) * scale  7.34 us
    cond x1, matrix products, on_device(): lax.cond(jnp.int32(0) <= qpos[rows - 1], lambda c: update(c, pieces), lam...  6.44 us
  transfers between devices with their start and end apart: 2, of which 2 were waited for; matrix products, arithmetic and copies ran while one was open for 4% of the time, Pallas kernels for 0%

commit v1 on v0

--- a/solution.py
+++ b/solution.py
@@ -100,7 +100,9 @@
     ).reshape(KVH * HD, HD)
     shard = sent_and_summed(partial_value, "blk", 0)
     prefix = carried_in(shard, "seg", add_terms, jnp.zeros_like(shard))
-    memory = lax.all_gather(prefix, "blk", axis=0, tiled=True)
+    memory = jnp.concatenate(
+        lax.all_to_all(jnp.stack([prefix] * lax.axis_size("blk")), "blk", 0, 0), axis=0
+    )
     retrieval = jnp.einsum(
         "rkgd,kde->kgre", sigma_map(q_heads), memory.reshape(KVH, HD, HD), precision=HIGH
     )

time: 170 us -> 172 us (1.012)
  the two profiles are of different devices: /device:TPU:3 before, /device:TPU:1 now
where the time goes in v1:
time: 172 us
  waiting for transfers between devices  71.9 us (42%)
  blocking collectives  34 us (20%)
  starting transfers between devices  22.6 us (13%)
  matrix products  15.6 us (9%)
  between operations  14.1 us (8%)
  local copies, waits for them, and re-layouts  8.83 us (5%)
  other arithmetic  4.63 us (3%)
    all_gather x1, waiting for transfers between devices, side_by_side(): filled = lax.all_gather(both, axis, axis=dim, tiled=True)  38 us
    all_to_all x1, blocking collectives, sent_and_summed(): parts = lax.all_to_all(split_up(shard, dim, peers), axis, 0, 0, tiled=True)  34 us
    all_to_all x1, waiting for transfers between devices, on_device(): lax.all_to_all(jnp.stack([prefix] * lax.axis_size('blk')), 'blk', 0, 0)  20.1 us
    all_to_all x1, waiting for transfers between devices, from_everyone(): return lax.all_to_all(copies, axis, split_axis=0, concat_axis=0, tiled=True)  13.8 us
    all_to_all x1, starting transfers between devices, from_everyone(): return lax.all_to_all(copies, axis, split_axis=0, concat_axis=0, tiled=True)  12.2 us
    all_to_all x1, starting transfers between devices, on_device(): lax.all_to_all(jnp.stack([prefix] * lax.axis_size('blk')), 'blk', 0, 0)  10.4 us
    dot_general x1, matrix products, update(): scores = jnp.einsum('rkgd,nkd->kgrn', q_heads, k_h, precision=HIGH) * scale  7.34 us
    cond x1, matrix products, on_device(): lax.cond(jnp.int32(0) <= qpos[rows - 1], lambda c: update(c, pieces), lam...  6.44 us
  transfers between devices with their start and end apart: 3, of which 3 were waited for; matrix products, arithmetic and copies ran while one was open for 4% of the time, Pallas kernels for 0%

profile of v1, /device:TPU:1, one launch (start us, length us, event | category | flops | bytes accessed | tf_op | source)
XLA Modules:
  0.0 172.0 jit_solution(13924990070404770850)
XLA Ops:
  6.5 0.0 all-gather.2.cloned.1.call-start
  6.5 1.0 copy.19
  7.5 1.0 copy.20
  8.5 0.7 pad_maximum_fusion
  9.3 0.0 all-gather.2.cloned.1.call-update
  9.3 0.9 exponential_select_fusion
  10.2 0.1 copy.34
  10.3 1.2 fusion.19
  11.5 34.0 %all_to_all.15 = f32[16,16,128]{2,1,0:T(8,128)S(1)} all-to-all(f32[16,16,128]{2,1,0:T(8,128)S(1)} %bitcast.58), channel_id=1, replica_groups=mesh['seg'=32,'blk'=16] {'blk'}, dimensions={0} | all-to-all | bytes 262144 | tf_op jit(solution)/shard_map/all_to_all | solution.py:27
  45.6 0.7 broadcast_in_dim.50
  46.3 12.2 %all-to-all-start.1 = ((f32[32,16,128]{2,1,0:T(8,128)}), f32[32,16,128]{2,1,0:T(8,128)S(1)}, u32[]{:S(2)}, u32[]{:S(2)}) async-start(f32[32,16,128]{2,1,0:T(8,128)} %broadcast_in_dim.50), calls=%async_computation.1 | async-start | bytes 524288 | tf_op jit(solution)/shard_map/all_to_all | solution.py:33
  58.5 13.8 %all-to-all-done.1 = f32[32,16,128]{2,1,0:T(8,128)S(1)} async-done(((f32[32,16,128]{2,1,0:T(8,128)}), f32[32,16,128]{2,1,0:T(8,128)S(1)}, u32[]{:S(2)}, u32[]{:S(2)}) %all-to-all-start.1) | async-done | bytes 262176 | tf_op jit(solution)/shard_map/all_to_all | solution.py:33
  72.3 0.1 broadcast_select_fusion
  72.5 0.7 stack.3
  73.1 10.4 %all-to-all-start.2 = ((f32[16,16,128]{2,1,0:T(8,128)}), f32[16,16,128]{2,1,0:T(8,128)S(1)}, u32[]{:S(2)}, u32[]{:S(2)}) async-start(f32[16,16,128]{2,1,0:T(8,128)} %stack.3), calls=%async_computation.2 | async-start | bytes 262144 | tf_op jit(solution)/shard_map/all_to_all | solution.py:104
  83.6 1.2 copy.16
  84.8 0.6 slice.45
  85.9 0.7 add_divide_fusion
  86.6 0.1 mul.40
  86.7 20.1 %all-to-all-done.2 = f32[16,16,128]{2,1,0:T(8,128)S(1)} async-done(((f32[16,16,128]{2,1,0:T(8,128)}), f32[16,16,128]{2,1,0:T(8,128)S(1)}, u32[]{:S(2)}, u32[]{:S(2)}) %all-to-all-start.2) | async-done | bytes 131104 | tf_op jit(solution)/shard_map/all_to_all | solution.py:104
  106.8 0.7 multiply_reduce_fusion
  107.5 38.0 %all-gather.2.cloned.1.call-done = f32[2048,512]{0,1:T(8,128)} async-done(((f32[128,512]{0,1:T(8,128)}), f32[2048,512]{0,1:T(8,128)}) %all-gather.2.cloned.1.call-update) | async-done | bytes 4194320 | tf_op jit(solution)/shard_map/all_gather | solution.py:16
  145.5 0.0 copy-start
  145.5 18.4 %conditional.1 = (f32[2,4,128]{2,1,0:T(4,128)S(1)}, f32[2,4,128,128]{2,3,1,0:T(8,128)S(1)}) conditional(s32[]{:T(128)} %bitcast.13, () %tuple.13, (s32[128]{0:T(128)S(1)}, f32[2048,512]{0,1:T(8,128)}, f32[128,2,4,128]{0,3,2,1:T(8,128)S(1)}) %tuple.25), branch_computations={%region_2.0_spmd, %region_3.6_spmd} | conditional | flops 6463683584 | bytes 39870992 | solution.py:93
  145.5 0.2 iota_compare_fusion
  145.7 2.5 %fusion.25 = (f32[2048,256]{0,1:T(8,128)S(1)}, f32[2048,256]{0,1:T(8,128)S(1)}) fusion(f32[2048,512]{0,1:T(8,128)} %get-tuple-element.15), kind=kLoop, calls=%fused_computation.44 | loop fusion | bytes 8388608 | tf_op jit(solution)/shard_map/split | solution.py:17
  148.2 7.3 %fusion = (f32[2,4,128]{2,1,0:T(4,128)S(1)}, f32[2,2048,128,4]{2,1,3,0:T(8,128)S(1)}) fusion(pred[128,2048]{0,1:T(8,128)(4,1)S(1)} %iota_compare_fusion, f32[2048,2,128,1]{0,2,3,1:T(8,128)S(1)} %bitcast.51, f32[128,2,4,128]{0,3,2,1:T(8,128)S(1)} %get-tuple-element.23), kind=kOutput, calls=%fused_computation.2 | convolution fusion | flops 3227515904 | bytes 11276288 | tf_op jit(solution)/shard_map/cond/branch_1_fun/rkgd,nkd->kgrn/dot_general | solution.py:77
  155.5 6.4 %fusion.3 = f32[2,4,128,128]{2,3,1,0:T(8,128)S(1)} fusion(f32[2048,2,128,1]{0,2,3,1:T(8,128)S(1)} %bitcast.55, f32[2,2048,128,4]{2,1,3,0:T(8,128)S(1)} %get-tuple-element.28, f32[2,4,128]{2,1,0:T(4,128)S(1)} %broadcast_maximum_fusion, pred[128,2048]{0,1:T(8,128)(4,1)S(1)} %iota_compare_fusion), kind=kOutput, calls=%fused_computation.5 | convolution fusion | flops 3227516928 | bytes 11276288 | tf_op jit(solution)/shard_map/cond | solution.py:93
  162.0 1.7 fusion.5
  163.9 0.0 copy-done
  164.0 0.2 multiply_add_fusion
  164.2 1.0 copy.23
  (11 shorter events, 0.1 us)
Async XLA Ops:
  6.5 139.0 %all-gather.2.cloned.1.call-start = ((), (), s32[]{:S(2)}) async-start(), calls=%async_computation.3 | async-start | bytes 4456448 | tf_op jit(solution)/shard_map/all_gather | solution.py:16
  46.3 26.0 %all-to-all-start.1 = ((f32[32,16,128]{2,1,0:T(8,128)}), f32[32,16,128]{2,1,0:T(8,128)S(1)}, u32[]{:S(2)}, u32[]{:S(2)}) async-start(f32[32,16,128]{2,1,0:T(8,128)} %broadcast_in_dim.50), calls=%async_computation.1 | async-start | bytes 524288 | tf_op jit(solution)/shard_map/all_to_all | solution.py:33
  73.1 33.6 %all-to-all-start.2 = ((f32[16,16,128]{2,1,0:T(8,128)}), f32[16,16,128]{2,1,0:T(8,128)S(1)}, u32[]{:S(2)}, u32[]{:S(2)}) async-start(f32[16,16,128]{2,1,0:T(8,128)} %stack.3), calls=%async_computation.2 | async-start | bytes 262144 | tf_op jit(solution)/shard_map/all_to_all | solution.py:104
  145.5 18.5 %copy-start = (f32[1024]{0:T(1024)S(1)}, f32[1024]{0:T(1024)}, u32[]{:S(2)}) copy-start(f32[1024]{0:T(1024)} %param.11) | copy-start | bytes 12292
Sparse Core Ops, SparseCore 0:
  10.5 134.9 all-gather.1
